TPU v7x, 128 devices: a whole 4x4x4 slice. The times are simulated.
128 devices in a mesh: row: 32 (over y, z, core), col: 4 (over x).
Axes of the slice: x: 4, y: 4, z: 4, core: 2. Of those that a mesh axis runs over, the one named last changes fastest.
Arguments:
- matrix: float32 [16384, 16, 512], P('row', 'col'), may hold values from -200 to 200, as said below
Outputs:
- factored: float32 [16384, 16, 512], P('row', 'col')
- upper_rows: float32 [2, 512, 16, 512], P(None, 'row', 'col')
Inputs may be any that keep to these rules, and one draw needn't show every extreme that they name: `matrix`: Real-valued entries; every panel has full column rank.
All inputs are finite; a program needn't handle non-finite values.
Results may differ from a plain program's by a relative error of at most 0.0001.
Values sent between devices are 32-bit elements; how exact they have to be, the bound alone decides.
A program may use at most 128 MiB of HBM per device.

v0:
```python
import jax
import jax.numpy as jnp
from jax import lax
from jax.sharding import PartitionSpec as P

PANELS = 2
HIGH = lax.Precision.HIGHEST


def spread(value, axis, root):
    mine = lax.axis_index(axis) == root
    return lax.psum(jnp.where(mine, value, jnp.zeros_like(value)), axis)


def right_solve(lower, block):
    eye = jnp.eye(lower.shape[0], dtype=jnp.float32)
    inverse = lax.linalg.triangular_solve(lower, eye, left_side=True, lower=True)
    return jnp.dot(block, inverse.T, precision=HIGH)


def gram_of(block):
    return jnp.dot(block.T, block, precision=HIGH)


def on_device(matrix):
    work = matrix
    row_dev, blocks, width = matrix.shape
    half = width // 2
    n_row = lax.axis_size("row")
    n_col = lax.axis_size("col")
    my_col = lax.axis_index("col")
    my_row = lax.axis_index("row")
    share = width // n_row
    scale = jnp.sqrt(jnp.float32(row_dev * n_row))
    number = jnp.arange(blocks) * n_col + my_col
    pieces = []
    for k in range(PANELS):
        root = k % n_col
        slot = k // n_col
        owner = my_col == root
        panel = work[:, slot, :]
        first = panel[:, :half]
        second = panel[:, half:]
        lower_one = jnp.linalg.cholesky(lax.psum(gram_of(first), "row"))
        basis_one = right_solve(lower_one, first)
        inner = lax.psum(jnp.dot(basis_one.T, second, precision=HIGH), "row")
        rest = second - jnp.dot(basis_one, inner, precision=HIGH)
        lower_two = jnp.linalg.cholesky(lax.psum(gram_of(rest), "row"))
        basis_two = right_solve(lower_two, rest)
        local_basis = jnp.concatenate([basis_one, basis_two], axis=1)
        top = jnp.concatenate([lower_one.T, inner], axis=1)
        bottom = jnp.concatenate([jnp.zeros((half, half), jnp.float32), lower_two.T], axis=1)
        upper = jnp.concatenate([top, bottom], axis=0)
        basis = spread(local_basis, "col", root)
        keep = (number > k).astype(jnp.float32)
        terms = jnp.einsum("rk,rbc->kbc", basis, work, precision=HIGH) * keep[None, :, None]
        weights = lax.psum(terms, "row")
        mine = lax.dynamic_slice_in_dim(weights, my_row * share, share, 0)
        work = work - jnp.einsum("rk,kbc->rbc", basis, weights, precision=HIGH)
        work = work.at[:, slot, :].set(jnp.where(owner, basis * scale, work[:, slot, :]))
        upper_share = lax.dynamic_slice_in_dim(upper, my_row * share, share, 0)
        mine = mine.at[:, slot, :].set(jnp.where(owner, upper_share, mine[:, slot, :]))
        pieces.append(mine)
    return (work, jnp.stack(pieces, axis=0))


def solution(mesh):
    placed = (P("row", "col", None),)
    return jax.shard_map(
        on_device,
        mesh=mesh,
        in_specs=placed,
        out_specs=(P("row", "col", None), P(None, "row", "col", None)),
        check_vma=False,
    )
```

profile of v0, /device:TPU:1, one launch (start us, length us, event | category | flops | bytes accessed | tf_op | source)
XLA Modules:
  0.0 1277.8 jit_solution(5746735367781790815)
XLA Ops:
  12.0 105.9 %all-reduce.14.cloned.1.call-done = f32[256,256]{0,1:T(8,128)} async-done(((f32[256,256]{0,1:T(8,128)}), f32[256,256]{0,1:T(8,128)}) %all-reduce.14.cloned.1.call-update) | async-done | bytes 262160 | tf_op jit(solution)/shard_map/psum | solution.py:44
  120.0 11.7 cholesky.214
  131.7 9.8 custom-call.17
  142.0 11.7 cholesky.231
  160.3 19.7 %custom-call.18 = f32[2,128,128]{1,2,0:T(8,128)S(1)} custom-call(f32[2,128,128]{2,1,0:T(8,128)S(1)} %get-tuple-element.78), custom_call_target="InvertDiagBlocksLowerTriangular" | custom-call | tf_op jit(solution)/shard_map/triangular_solve/custom-call.0 | solution.py:17
  183.3 102.1 %all-reduce.16.cloned.1.call-done = f32[256,256]{0,1:T(8,128)} async-done(((f32[256,256]{0,1:T(8,128)}), f32[256,256]{0,1:T(8,128)}) %all-reduce.16.cloned.1.call-update) | async-done | bytes 262160 | tf_op jit(solution)/shard_map/psum | solution.py:46
  289.6 101.7 %all-reduce.18.cloned.1.call-done = f32[256,256]{0,1:T(8,128)} async-done(((f32[256,256]{0,1:T(8,128)}), f32[256,256]{0,1:T(8,128)}) %all-reduce.18.cloned.1.call-update) | async-done | bytes 262160 | tf_op jit(solution)/shard_map/psum | solution.py:48
  393.4 11.7 cholesky.248
  405.1 9.8 custom-call.19
  415.6 11.7 cholesky.265
  434.4 19.7 %custom-call.20 = f32[2,128,128]{1,2,0:T(8,128)S(1)} custom-call(f32[2,128,128]{2,1,0:T(8,128)S(1)} %get-tuple-element.79), custom_call_target="InvertDiagBlocksLowerTriangular" | custom-call | tf_op jit(solution)/shard_map/triangular_solve/custom-call.0 | solution.py:17
  456.8 5.2 copy.42
  462.1 38.5 %all-reduce.20.cloned.1.call-done = f32[512,512]{0,1:T(8,128)} async-done(((f32[512,512]{0,1:T(8,128)}), f32[512,512]{0,1:T(8,128)}) %all-reduce.20.cloned.1.call-update) | async-done | bytes 1048592 | tf_op jit(solution)/shard_map/psum | solution.py:12
  500.6 10.2 convolution_multiply_fusion.1
  510.8 114.6 %all-reduce.22.cloned.1.call-done = f32[512,4,512]{0,2,1:T(8,128)} async-done(((f32[512,4,512]{0,2,1:T(8,128)}), f32[512,4,512]{0,2,1:T(8,128)}) %all-reduce.22.cloned.1.call-update) | async-done | bytes 4194320 | tf_op jit(solution)/shard_map/psum | solution.py:57
  625.4 9.2 convolution_subtract_fusion.1
  638.7 101.8 %all-reduce.24.cloned.1.call-done = f32[256,256]{0,1:T(8,128)} async-done(((f32[256,256]{0,1:T(8,128)}), f32[256,256]{0,1:T(8,128)}) %all-reduce.24.cloned.1.call-update) | async-done | bytes 262160 | tf_op jit(solution)/shard_map/psum | solution.py:44
  742.5 11.7 cholesky.282
  754.3 9.8 custom-call.21
  764.6 11.7 cholesky.299
  783.5 19.7 %custom-call.22 = f32[2,128,128]{1,2,0:T(8,128)S(1)} custom-call(f32[2,128,128]{2,1,0:T(8,128)S(1)} %get-tuple-element.80), custom_call_target="InvertDiagBlocksLowerTriangular" | custom-call | tf_op jit(solution)/shard_map/triangular_solve/custom-call.0 | solution.py:17
  806.1 102.1 %all-reduce.26.cloned.1.call-done = f32[256,256]{0,1:T(8,128)} async-done(((f32[256,256]{0,1:T(8,128)}), f32[256,256]{0,1:T(8,128)}) %all-reduce.26.cloned.1.call-update) | async-done | bytes 262160 | tf_op jit(solution)/shard_map/psum | solution.py:46
  911.4 102.1 %all-reduce.28.cloned.1.call-done = f32[256,256]{0,1:T(8,128)} async-done(((f32[256,256]{0,1:T(8,128)}), f32[256,256]{0,1:T(8,128)}) %all-reduce.28.cloned.1.call-update) | async-done | bytes 262160 | tf_op jit(solution)/shard_map/psum | solution.py:48
  1015.5 11.7 cholesky.316
  1027.3 9.8 custom-call.23
  1037.8 11.7 cholesky.333
  1057.0 19.7 %custom-call.24 = f32[2,128,128]{1,2,0:T(8,128)S(1)} custom-call(f32[2,128,128]{2,1,0:T(8,128)S(1)} %get-tuple-element.81), custom_call_target="InvertDiagBlocksLowerTriangular" | custom-call | tf_op jit(solution)/shard_map/triangular_solve/custom-call.0 | solution.py:17
  1080.4 42.7 %all-reduce.30.cloned.1.call-done = f32[512,512]{0,1:T(8,128)} async-done(((f32[512,512]{0,1:T(8,128)}), f32[512,512]{0,1:T(8,128)}) %all-reduce.30.cloned.1.call-update) | async-done | bytes 1048592 | tf_op jit(solution)/shard_map/psum | solution.py:12
  1123.1 10.2 convolution_multiply_fusion
  1137.6 110.4 %all-reduce.32.cloned.1.call-done = f32[512,4,512]{0,2,1:T(8,128)} async-done(((f32[512,4,512]{0,2,1:T(8,128)}), f32[512,4,512]{0,2,1:T(8,128)}) %all-reduce.32.cloned.1.call-update) | async-done | bytes 4194320 | tf_op jit(solution)/shard_map/psum | solution.py:57
  1252.2 10.5 convolution_subtract_fusion
  1265.1 5.4 copy.60
  (161 shorter events, 89.0 us)
Async XLA Ops:
  7.2 110.7 %all-reduce.14.cloned.1.call-start = ((), (), s32[]{:S(2)}) async-start(), calls=%async_computation | async-start | bytes 524288 | tf_op jit(solution)/shard_map/psum | solution.py:44
  11.9 273.5 %all-reduce.16.cloned.1.call-start = ((), (), s32[]{:S(2)}) async-start(), calls=%async_computation.1 | async-start | bytes 524288 | tf_op jit(solution)/shard_map/psum | solution.py:46
  183.3 208.0 %all-reduce.18.cloned.1.call-start = ((), (), s32[]{:S(2)}) async-start(), calls=%async_computation.2 | async-start | bytes 524288 | tf_op jit(solution)/shard_map/psum | solution.py:48
  289.1 211.4 %all-reduce.20.cloned.1.call-start = ((), (), s32[]{:S(2)}) async-start(), calls=%async_computation.3 | async-start | bytes 2097152 | tf_op jit(solution)/shard_map/psum | solution.py:12
  456.8 168.6 %all-reduce.22.cloned.1.call-start = ((), (), s32[]{:S(2)}) async-start(), calls=%async_computation.4 | async-start | bytes 8388608 | tf_op jit(solution)/shard_map/psum | solution.py:57
  510.7 114.7 %copy-start.2 = (f32[512,512]{0,1:T(8,128)S(1)}, f32[512,512]{0,1:T(8,128)}, u32[]{:S(2)}) copy-start(f32[512,512]{0,1:T(8,128)} %all-reduce.20.cloned.1.call-done) | copy-start | bytes 3145732
  510.7 229.7 %all-reduce.24.cloned.1.call-start = ((), (), s32[]{:S(2)}) async-start(), calls=%async_computation.5 | async-start | bytes 524288 | tf_op jit(solution)/shard_map/psum | solution.py:44
  634.6 2.0 copy-start
  638.2 270.0 %all-reduce.26.cloned.1.call-start = ((), (), s32[]{:S(2)}) async-start(), calls=%async_computation.6 | async-start | bytes 524288 | tf_op jit(solution)/shard_map/psum | solution.py:46
  806.1 207.4 %all-reduce.28.cloned.1.call-start = ((), (), s32[]{:S(2)}) async-start(), calls=%async_computation.7 | async-start | bytes 524288 | tf_op jit(solution)/shard_map/psum | solution.py:48
  911.2 212.0 %all-reduce.30.cloned.1.call-start = ((), (), s32[]{:S(2)}) async-start(), calls=%async_computation.8 | async-start | bytes 2097152 | tf_op jit(solution)/shard_map/psum | solution.py:12
  1079.3 168.7 %all-reduce.32.cloned.1.call-start = ((), (), s32[]{:S(2)}) async-start(), calls=%async_computation.9 | async-start | bytes 8388608 | tf_op jit(solution)/shard_map/psum | solution.py:57
  1133.3 0.9 copy-start.3
  1133.3 114.7 %copy-start.4 = (f32[256,256]{0,1:T(8,128)S(1)}, f32[256,256]{0,1:T(8,128)}, u32[]{:S(2)}) copy-start(f32[256,256]{0,1:T(8,128)} %all-reduce.26.cloned.1.call-done) | copy-start | bytes 786436
  1133.3 114.7 %copy-start.5 = (f32[256,256]{0,1:T(8,128)S(1)}, f32[256,256]{0,1:T(8,128)}, u32[]{:S(2)}) copy-start(f32[256,256]{0,1:T(8,128)} %get-tuple-element.132) | copy-start | bytes 786436
  1133.3 114.7 %copy-start.6 = (f32[256,256]{0,1:T(8,128)S(1)}, f32[256,256]{0,1:T(8,128)}, u32[]{:S(2)}) copy-start(f32[256,256]{0,1:T(8,128)} %get-tuple-element.130) | copy-start | bytes 786436
  1135.6 116.6 %copy-start.1 = (f32[512,512]{0,1:T(8,128)S(1)}, f32[512,512]{0,1:T(8,128)}, u32[]{:S(2)}) copy-start(f32[512,512]{0,1:T(8,128)} %all-reduce.30.cloned.1.call-done) | copy-start | bytes 3145732
Sparse Core Ops, SparseCore 0:
  12.0 105.7 all-reduce.13
  183.4 102.0 all-reduce.15
  289.3 101.9 all-reduce.17
  456.9 43.6 all-reduce.19
  510.9 114.5 all-reduce.21
  638.4 102.0 all-reduce.23
  806.2 101.9 all-reduce.25
  911.4 101.9 all-reduce.27
  1079.4 43.6 all-reduce.29
  1133.5 114.5 all-reduce.31
where the time goes:
time: 1290 us; the launch traced here: 1280 us
  waiting for transfers between devices  922 us (71%)
  other arithmetic  229 us (18%)
  matrix products  60.8 us (5%)
  local copies, waits for them, and re-layouts  43 us (3%)
  between operations  20.3 us (2%)
    psum x2, waiting for transfers between devices, on_device(): weights = lax.psum(terms, 'row')  225 us
    psum x2, waiting for transfers between devices, on_device(): lower_one = jnp.linalg.cholesky(lax.psum(gram_of(first), 'row'))  208 us
    psum x2, waiting for transfers between devices, on_device(): inner = lax.psum(jnp.dot(basis_one.T, second, precision=HIGH), 'row')  204 us
    psum x2, waiting for transfers between devices, on_device(): lower_two = jnp.linalg.cholesky(lax.psum(gram_of(rest), 'row'))  204 us
    psum x2, waiting for transfers between devices, spread(): return lax.psum(jnp.where(mine, value, jnp.zeros_like(value)), axis)  81.2 us
    another operation x5, other arithmetic, right_solve(): lax.linalg.triangular_solve(lower, eye, left_side=True, lower=True)  78.7 us
    another operation x14, other arithmetic, on_device(): lower_two = jnp.linalg.cholesky(lax.psum(gram_of(rest), 'row'))  69.3 us
    another operation x13, other arithmetic, on_device(): lower_one = jnp.linalg.cholesky(lax.psum(gram_of(first), 'row'))  68.6 us
  transfers between devices with their start and end apart: 10, of which 10 were waited for; matrix products, arithmetic and copies ran while one was open for 1% of the time, Pallas kernels for 0%

commit v1 on v0

--- a/solution.py
+++ b/solution.py
@@ -54,7 +54,11 @@
         basis = spread(local_basis, "col", root)
         keep = (number > k).astype(jnp.float32)
         terms = jnp.einsum("rk,rbc->kbc", basis, work, precision=HIGH) * keep[None, :, None]
-        weights = lax.psum(terms, "row")
+        weights = terms
+        for hop in (1, 2, 4, 8, 16):
+            weights = weights + lax.ppermute(
+                weights, "row", [(dev, dev ^ hop) for dev in range(32)]
+            )
         mine = lax.dynamic_slice_in_dim(weights, my_row * share, share, 0)
         work = work - jnp.einsum("rk,kbc->rbc", basis, weights, precision=HIGH)
         work = work.at[:, slot, :].set(jnp.where(owner, basis * scale, work[:, slot, :]))

time: 1290 us -> 1830 us (1.42)
  waiting for transfers between devices: 922 us -> 1430 us
  starting transfers between devices: 1.39 us -> 23.3 us
    ppermute x0 -> x10, waiting for transfers between devices: none -> 724 us  [on_device(): lax.ppermute(weights, 'row', [(dev, dev ^ hop) for dev in range(32)])]
    psum x2 -> x0, waiting for transfers between devices: 225 us -> none  [on_device(): weights = lax.psum(terms, 'row')]
    ppermute x0 -> x10, starting transfers between devices: none -> 22.2 us  [on_device(): lax.ppermute(weights, 'row', [(dev, dev ^ hop) for dev in range(32)])]
  transfers between devices with their start and end apart: 10 -> 18, of which waited for: 10 -> 18; matrix products, arithmetic and copies ran while one was open for 1% -> 1% of each run, Pallas kernels for 0% -> 0%
where the time goes in v1:
time: 1830 us; the launch traced here: 1810 us
  waiting for transfers between devices  1430 us (78%)
  other arithmetic  244 us (13%)
  matrix products  56.2 us (3%)
  local copies, waits for them, and re-layouts  42.4 us (2%)
  starting transfers between devices  23.3 us (1%)
  between operations  20.5 us (1%)
    ppermute x10, waiting for transfers between devices, on_device(): lax.ppermute(weights, 'row', [(dev, dev ^ hop) for dev in range(32)])  724 us
    psum x2, waiting for transfers between devices, on_device(): lower_one = jnp.linalg.cholesky(lax.psum(gram_of(first), 'row'))  212 us
    psum x2, waiting for transfers between devices, on_device(): inner = lax.psum(jnp.dot(basis_one.T, second, precision=HIGH), 'row')  204 us
    psum x2, waiting for transfers between devices, on_device(): lower_two = jnp.linalg.cholesky(lax.psum(gram_of(rest), 'row'))  204 us
    psum x2, waiting for transfers between devices, spread(): return lax.psum(jnp.where(mine, value, jnp.zeros_like(value)), axis)  81.2 us
    another operation x5, other arithmetic, right_solve(): lax.linalg.triangular_solve(lower, eye, left_side=True, lower=True)  78.7 us
    another operation x14, other arithmetic, on_device(): lower_two = jnp.linalg.cholesky(lax.psum(gram_of(rest), 'row'))  69.3 us
    another operation x13, other arithmetic, on_device(): lower_one = jnp.linalg.cholesky(lax.psum(gram_of(first), 'row'))  68.6 us
  transfers between devices with their start and end apart: 18, of which 18 were waited for; matrix products, arithmetic and copies ran while one was open for 1% of the time, Pallas kernels for 0%

profile of v1, /device:TPU:1, one launch (start us, length us, event | category | flops | bytes accessed | tf_op | source)
XLA Modules:
  0.0 1813.3 jit_solution(5752688161945131258)
XLA Ops:
  12.0 105.9 %all-reduce.12.cloned.1.call-done = f32[256,256]{0,1:T(8,128)} async-done(((f32[256,256]{0,1:T(8,128)}), f32[256,256]{0,1:T(8,128)}) %all-reduce.12.cloned.1.call-update) | async-done | bytes 262160 | tf_op jit(solution)/shard_map/psum | solution.py:44
  120.0 11.7 cholesky.214
  131.7 9.8 custom-call.17
  142.0 11.7 cholesky.231
  160.3 19.7 %custom-call.18 = f32[2,128,128]{1,2,0:T(8,128)S(1)} custom-call(f32[2,128,128]{2,1,0:T(8,128)S(1)} %get-tuple-element.78), custom_call_target="InvertDiagBlocksLowerTriangular" | custom-call | tf_op jit(solution)/shard_map/triangular_solve/custom-call.0 | solution.py:17
  183.3 102.1 %all-reduce.14.cloned.1.call-done = f32[256,256]{0,1:T(8,128)} async-done(((f32[256,256]{0,1:T(8,128)}), f32[256,256]{0,1:T(8,128)}) %all-reduce.14.cloned.1.call-update) | async-done | bytes 262160 | tf_op jit(solution)/shard_map/psum | solution.py:46
  289.3 101.9 %all-reduce.16.cloned.1.call-done = f32[256,256]{0,1:T(8,128)} async-done(((f32[256,256]{0,1:T(8,128)}), f32[256,256]{0,1:T(8,128)}) %all-reduce.16.cloned.1.call-update) | async-done | bytes 262160 | tf_op jit(solution)/shard_map/psum | solution.py:48
  393.3 11.7 cholesky.248
  405.0 9.8 custom-call.19
  415.5 11.7 cholesky.265
  434.6 19.7 %custom-call.20 = f32[2,128,128]{1,2,0:T(8,128)S(1)} custom-call(f32[2,128,128]{2,1,0:T(8,128)S(1)} %get-tuple-element.79), custom_call_target="InvertDiagBlocksLowerTriangular" | custom-call | tf_op jit(solution)/shard_map/triangular_solve/custom-call.0 | solution.py:17
  462.3 38.5 %all-reduce.18.cloned.1.call-done = f32[512,512]{0,1:T(8,128)} async-done(((f32[512,512]{0,1:T(8,128)}), f32[512,512]{0,1:T(8,128)}) %all-reduce.18.cloned.1.call-update) | async-done | bytes 1048592 | tf_op jit(solution)/shard_map/psum | solution.py:12
  521.4 90.5 %collective-permute-done.1 = f32[512,4,512]{0,2,1:T(8,128)S(1)} collective-permute-done((f32[512,4,512]{0,2,1:T(8,128)S(1)}, f32[512,4,512]{0,2,1:T(8,128)S(1)}, u32[]{:S(2)}, u32[]{:S(2)}) %collective-permute-start.1) | collective-permute-done | bytes 4194336 | tf_op jit(solution)/shard_map/ppermute | solution.py:59
  615.8 89.5 %collective-permute-done.2 = f32[512,4,512]{0,2,1:T(8,128)S(1)} collective-permute-done((f32[512,4,512]{0,2,1:T(8,128)S(1)}, f32[512,4,512]{0,2,1:T(8,128)S(1)}, u32[]{:S(2)}, u32[]{:S(2)}) %collective-permute-start.2) | collective-permute-done | bytes 4194336 | tf_op jit(solution)/shard_map/ppermute | solution.py:59
  707.8 88.8 %collective-permute-done.3 = f32[512,4,512]{0,2,1:T(8,128)S(1)} collective-permute-done((f32[512,4,512]{0,2,1:T(8,128)S(1)}, f32[512,4,512]{0,2,1:T(8,128)S(1)}, u32[]{:S(2)}, u32[]{:S(2)}) %collective-permute-start.3) | collective-permute-done | bytes 4194336 | tf_op jit(solution)/shard_map/ppermute | solution.py:59
  800.5 88.0 %collective-permute-done.4 = f32[512,4,512]{0,2,1:T(8,128)S(1)} collective-permute-done((f32[512,4,512]{0,2,1:T(8,128)S(1)}, f32[512,4,512]{0,2,1:T(8,128)S(1)}, u32[]{:S(2)}, u32[]{:S(2)}) %collective-permute-start.4) | collective-permute-done | bytes 4194336 | tf_op jit(solution)/shard_map/ppermute | solution.py:59
  900.7 106.3 %all-reduce.20.cloned.1.call-done = f32[256,256]{0,1:T(8,128)} async-done(((f32[256,256]{0,1:T(8,128)}), f32[256,256]{0,1:T(8,128)}) %all-reduce.20.cloned.1.call-update) | async-done | bytes 262160 | tf_op jit(solution)/shard_map/psum | solution.py:44
  1009.1 11.7 cholesky.282
  1031.2 11.7 cholesky.299
  1050.1 19.7 %custom-call.22 = f32[2,128,128]{1,2,0:T(8,128)S(1)} custom-call(f32[2,128,128]{2,1,0:T(8,128)S(1)} %get-tuple-element.80), custom_call_target="InvertDiagBlocksLowerTriangular" | custom-call | tf_op jit(solution)/shard_map/triangular_solve/custom-call.0 | solution.py:17
  1072.7 102.0 %all-reduce.22.cloned.1.call-done = f32[256,256]{0,1:T(8,128)} async-done(((f32[256,256]{0,1:T(8,128)}), f32[256,256]{0,1:T(8,128)}) %all-reduce.22.cloned.1.call-update) | async-done | bytes 262160 | tf_op jit(solution)/shard_map/psum | solution.py:46
  1177.9 102.1 %all-reduce.24.cloned.1.call-done = f32[256,256]{0,1:T(8,128)} async-done(((f32[256,256]{0,1:T(8,128)}), f32[256,256]{0,1:T(8,128)}) %all-reduce.24.cloned.1.call-update) | async-done | bytes 262160 | tf_op jit(solution)/shard_map/psum | solution.py:48
  1282.1 11.7 cholesky.316
  1293.8 9.8 custom-call.23
  1304.4 11.7 cholesky.333
  1323.5 19.7 %custom-call.24 = f32[2,128,128]{1,2,0:T(8,128)S(1)} custom-call(f32[2,128,128]{2,1,0:T(8,128)S(1)} %get-tuple-element.81), custom_call_target="InvertDiagBlocksLowerTriangular" | custom-call | tf_op jit(solution)/shard_map/triangular_solve/custom-call.0 | solution.py:17
  1346.9 42.7 %all-reduce.26.cloned.1.call-done = f32[512,512]{0,1:T(8,128)} async-done(((f32[512,512]{0,1:T(8,128)}), f32[512,512]{0,1:T(8,128)}) %all-reduce.26.cloned.1.call-update) | async-done | bytes 1048592 | tf_op jit(solution)/shard_map/psum | solution.py:12
  1410.2 90.5 %collective-permute-done.6 = f32[512,4,512]{0,2,1:T(8,128)S(1)} collective-permute-done((f32[512,4,512]{0,2,1:T(8,128)S(1)}, f32[512,4,512]{0,2,1:T(8,128)S(1)}, u32[]{:S(2)}, u32[]{:S(2)}) %collective-permute-start.6) | collective-permute-done | bytes 4194336 | tf_op jit(solution)/shard_map/ppermute | solution.py:59
  1504.7 89.5 %collective-permute-done.7 = f32[512,4,512]{0,2,1:T(8,128)S(1)} collective-permute-done((f32[512,4,512]{0,2,1:T(8,128)S(1)}, f32[512,4,512]{0,2,1:T(8,128)S(1)}, u32[]{:S(2)}, u32[]{:S(2)}) %collective-permute-start.7) | collective-permute-done | bytes 4194336 | tf_op jit(solution)/shard_map/ppermute | solution.py:59
  1596.8 88.8 %collective-permute-done.8 = f32[512,4,512]{0,2,1:T(8,128)S(1)} collective-permute-done((f32[512,4,512]{0,2,1:T(8,128)S(1)}, f32[512,4,512]{0,2,1:T(8,128)S(1)}, u32[]{:S(2)}, u32[]{:S(2)}) %collective-permute-start.8) | collective-permute-done | bytes 4194336 | tf_op jit(solution)/shard_map/ppermute | solution.py:59
  1694.6 85.0 %collective-permute-done.9 = f32[512,4,512]{0,2,1:T(8,128)} collective-permute-done((f32[512,4,512]{0,2,1:T(8,128)}, f32[512,4,512]{0,2,1:T(8,128)}, u32[]{:S(2)}, u32[]{:S(2)}) %collective-permute-start.9) | collective-permute-done | bytes 4194336 | tf_op jit(solution)/shard_map/ppermute | solution.py:59
  1787.7 10.5 convolution_subtract_fusion
  (191 shorter events, 184.2 us)
Async XLA Ops:
  7.2 110.7 %all-reduce.12.cloned.1.call-start = ((), (), s32[]{:S(2)}) async-start(), calls=%async_computation | async-start | bytes 524288 | tf_op jit(solution)/shard_map/psum | solution.py:44
  11.9 273.4 %all-reduce.14.cloned.1.call-start = ((), (), s32[]{:S(2)}) async-start(), calls=%async_computation.1 | async-start | bytes 524288 | tf_op jit(solution)/shard_map/psum | solution.py:46
  183.2 208.0 %all-reduce.16.cloned.1.call-start = ((), (), s32[]{:S(2)}) async-start(), calls=%async_computation.2 | async-start | bytes 524288 | tf_op jit(solution)/shard_map/psum | solution.py:48
  289.0 211.7 %all-reduce.18.cloned.1.call-start = ((), (), s32[]{:S(2)}) async-start(), calls=%async_computation.3 | async-start | bytes 2097152 | tf_op jit(solution)/shard_map/psum | solution.py:12
  457.0 550.1 %all-reduce.20.cloned.1.call-start = ((), (), s32[]{:S(2)}) async-start(), calls=%async_computation.4 | async-start | bytes 524288 | tf_op jit(solution)/shard_map/psum | solution.py:44
  509.7 9.3 collective-permute-start
  520.0 91.8 %collective-permute-start.1 = (f32[512,4,512]{0,2,1:T(8,128)S(1)}, f32[512,4,512]{0,2,1:T(8,128)S(1)}, u32[]{:S(2)}, u32[]{:S(2)}) collective-permute-start(f32[512,4,512]{0,2,1:T(8,128)S(1)} %add.102), channel_id=1, source_target_pairs={{0,8},{4,12},{8,0},{12,4},{16,24},{20,28},{24,16},{28,20},{32,40},... | collective-permute-start | bytes 12582920 | tf_op jit(solution)/shard_map/ppermute | solution.py:59
  612.9 92.5 %collective-permute-start.2 = (f32[512,4,512]{0,2,1:T(8,128)S(1)}, f32[512,4,512]{0,2,1:T(8,128)S(1)}, u32[]{:S(2)}, u32[]{:S(2)}) collective-permute-start(f32[512,4,512]{0,2,1:T(8,128)S(1)} %add.103), channel_id=1, source_target_pairs={{0,16},{4,20},{8,24},{12,28},{16,0},{20,4},{24,8},{28,12},{32,48},... | collective-permute-start | bytes 12582920 | tf_op jit(solution)/shard_map/ppermute | solution.py:59
  706.4 90.3 %collective-permute-start.3 = (f32[512,4,512]{0,2,1:T(8,128)S(1)}, f32[512,4,512]{0,2,1:T(8,128)S(1)}, u32[]{:S(2)}, u32[]{:S(2)}) collective-permute-start(f32[512,4,512]{0,2,1:T(8,128)S(1)} %add.104), channel_id=1, source_target_pairs={{0,32},{4,36},{8,40},{12,44},{16,48},{20,52},{24,56},{28,60},{32,0... | collective-permute-start | bytes 12582920 | tf_op jit(solution)/shard_map/ppermute | solution.py:59
  797.7 91.8 %copy-start.1 = (f32[512,4,512]{0,2,1:T(8,128)S(1)}, f32[512,4,512]{0,2,1:T(8,128)}, u32[]{:S(2)}) copy-start(f32[512,4,512]{0,2,1:T(8,128)} %copy.42) | copy-start | bytes 12582916
  797.7 91.8 %copy-start.5 = (f32[512,512]{0,1:T(8,128)S(1)}, f32[512,512]{0,1:T(8,128)}, u32[]{:S(2)}) copy-start(f32[512,512]{0,1:T(8,128)} %all-reduce.18.cloned.1.call-done) | copy-start | bytes 3145732
  797.7 90.8 %collective-permute-start.4 = (f32[512,4,512]{0,2,1:T(8,128)S(1)}, f32[512,4,512]{0,2,1:T(8,128)S(1)}, u32[]{:S(2)}, u32[]{:S(2)}) collective-permute-start(f32[512,4,512]{0,2,1:T(8,128)S(1)} %add.105), channel_id=1, source_target_pairs={{0,64},{4,68},{8,72},{12,76},{16,80},{20,84},{24,88},{28,92},{32,9... | collective-permute-start | bytes 12582920 | tf_op jit(solution)/shard_map/ppermute | solution.py:59
  889.5 7.2 copy-start.2
  896.7 2.0 copy-start
  900.3 274.5 %all-reduce.22.cloned.1.call-start = ((), (), s32[]{:S(2)}) async-start(), calls=%async_computation.5 | async-start | bytes 524288 | tf_op jit(solution)/shard_map/psum | solution.py:46
  1072.7 207.3 %all-reduce.24.cloned.1.call-start = ((), (), s32[]{:S(2)}) async-start(), calls=%async_computation.6 | async-start | bytes 524288 | tf_op jit(solution)/shard_map/psum | solution.py:48
  1177.7 211.9 %all-reduce.26.cloned.1.call-start = ((), (), s32[]{:S(2)}) async-start(), calls=%async_computation.7 | async-start | bytes 2097152 | tf_op jit(solution)/shard_map/psum | solution.py:12
  1398.5 9.3 collective-permute-start.5
  1408.8 91.8 %collective-permute-start.6 = (f32[512,4,512]{0,2,1:T(8,128)S(1)}, f32[512,4,512]{0,2,1:T(8,128)S(1)}, u32[]{:S(2)}, u32[]{:S(2)}) collective-permute-start(f32[512,4,512]{0,2,1:T(8,128)S(1)} %add.107), channel_id=1, source_target_pairs={{0,8},{4,12},{8,0},{12,4},{16,24},{20,28},{24,16},{28,20},{32,40},... | collective-permute-start | bytes 12582920 | tf_op jit(solution)/shard_map/ppermute | solution.py:59
  1501.7 92.5 %collective-permute-start.7 = (f32[512,4,512]{0,2,1:T(8,128)S(1)}, f32[512,4,512]{0,2,1:T(8,128)S(1)}, u32[]{:S(2)}, u32[]{:S(2)}) collective-permute-start(f32[512,4,512]{0,2,1:T(8,128)S(1)} %add.108), channel_id=1, source_target_pairs={{0,16},{4,20},{8,24},{12,28},{16,0},{20,4},{24,8},{28,12},{32,48},... | collective-permute-start | bytes 12582920 | tf_op jit(solution)/shard_map/ppermute | solution.py:59
  1595.2 96.1 %copy-start.6 = (f32[256,256]{0,1:T(8,128)S(1)}, f32[256,256]{0,1:T(8,128)}, u32[]{:S(2)}) copy-start(f32[256,256]{0,1:T(8,128)} %all-reduce.14.cloned.1.call-done) | copy-start | bytes 786436
  1595.2 90.4 %collective-permute-start.8 = (f32[512,4,512]{0,2,1:T(8,128)S(1)}, f32[512,4,512]{0,2,1:T(8,128)S(1)}, u32[]{:S(2)}, u32[]{:S(2)}) collective-permute-start(f32[512,4,512]{0,2,1:T(8,128)S(1)} %add.109), channel_id=1, source_target_pairs={{0,32},{4,36},{8,40},{12,44},{16,48},{20,52},{24,56},{28,60},{32,0... | collective-permute-start | bytes 12582920 | tf_op jit(solution)/shard_map/ppermute | solution.py:59
  1688.6 91.0 %collective-permute-start.9 = (f32[512,4,512]{0,2,1:T(8,128)}, f32[512,4,512]{0,2,1:T(8,128)}, u32[]{:S(2)}, u32[]{:S(2)}) collective-permute-start(f32[512,4,512]{0,2,1:T(8,128)} %add.110), channel_id=1, source_target_pairs={{0,64},{4,68},{8,72},{12,76},{16,80},{20,84},{24,88},{28,92},{32,9... | collective-permute-start | bytes 12582920 | tf_op jit(solution)/shard_map/ppermute | solution.py:59
  1694.6 91.5 %copy-start.7 = (f32[256,256]{0,1:T(8,128)S(1)}, f32[256,256]{0,1:T(8,128)}, u32[]{:S(2)}) copy-start(f32[256,256]{0,1:T(8,128)} %all-reduce.22.cloned.1.call-done) | copy-start | bytes 786436
  1694.6 91.5 %copy-start.8 = (f32[256,256]{0,1:T(8,128)S(1)}, f32[256,256]{0,1:T(8,128)}, u32[]{:S(2)}) copy-start(f32[256,256]{0,1:T(8,128)} %get-tuple-element.132) | copy-start | bytes 786436
  1694.6 91.4 %copy-start.9 = (f32[256,256]{0,1:T(8,128)S(1)}, f32[256,256]{0,1:T(8,128)}, u32[]{:S(2)}) copy-start(f32[256,256]{0,1:T(8,128)} %get-tuple-element.130) | copy-start | bytes 786436
  1784.1 1.9 copy-start.3
  1784.1 3.6 copy-start.4
Sparse Core Ops, SparseCore 0:
  12.1 105.7 all-reduce.11
  183.3 101.9 all-reduce.13
  289.2 101.9 all-reduce.15
  457.1 43.6 all-reduce.17
  900.4 106.5 all-reduce.19
  1072.8 101.9 all-reduce.21
  1178.0 101.9 all-reduce.23
  1345.9 43.6 all-reduce.25
